TPU v7x, 32 devices: a whole 2x2x4 slice. The times are simulated.
32 devices in a mesh: groups: 2 (over y), tm: 16 (over z, x, core).
Axes of the slice: x: 2, y: 2, z: 4, core: 2. Of those that a mesh axis runs over, the one named last changes fastest.
Arguments:
- unit_ids: int32 [24576], P(('groups', 'tm')), parts along dimension 0, may hold values from 0 to 999
- durations: int32 [24576], P(('groups', 'tm')), parts along dimension 0, may hold values from 1 to 8, 24576 in all
- unit_table: bfloat16 [1000, 128], replicated, may hold values from -6 to 6
- pre_weight: bfloat16 [384, 512], replicated, may hold values from -0.3125 to 0.3125
- up_weight: bfloat16 [512, 1280], replicated, may hold values from -0.25 to 0.25
- post_weight: float32 [256], replicated, may hold values from -0.375 to 0.375
- disc_taps: float32 [5, 5, 32], replicated, may hold values from -2.5 to 2.5
- disc_out: float32 [5, 32], replicated, may hold values from -1 to 1
Outputs:
- waveform: float32 [245760], P(('groups', 'tm')), parts along dimension 0
- wave_grad: float32 [245760], P(('groups', 'tm')), parts along dimension 0
- grad_pre: float32 [768, 512], P(('groups', 'tm')), parts along dimension 0
- grad_up: float32 [1024, 1280], P(('groups', 'tm')), parts along dimension 0
There are 2 independent parts, one for each index of `groups`. A program takes and returns all parts, laid end to end along the dimension named above; an argument that names none is the same for every part. Nothing has to cross between parts.
Inputs may be any that keep to these rules, and one draw needn't show every extreme that they name: durations sum to 24576 in each utterance batch (index of groups).
All inputs are finite; a program needn't handle non-finite values.
Results may differ from a plain program's by a relative error of at most 0.0055.
Values sent between devices are 32-bit elements; how exact they have to be, the bound alone decides.
A program may use at most 128 MiB of HBM per device.

v0:
```python
import functools

import jax
import jax.numpy as jnp
import numpy as np
from jax import lax
from jax.experimental import pallas as pl
from jax.experimental.pallas import tpu as pltpu
from jax.sharding import PartitionSpec as P

C = 256
UP = 5
KD = 5
F_DEV = 1536
HALO = 16
EXT = F_DEV + 2 * HALO
FRONT = 224
BACK = 256
LANES = 1664
CHUNK = 128
TURNS = 10
PAIRS = 32
CHANNELS = 160

period_list = (2, 3, 5, 7, 11)
log_two = 0.6931471805599453
MESH = pl.DeviceIdType.MESH
VMEM = pltpu.VMEM


def leaky_relu(v):
    return 0.1 * v + 0.9 * (jnp.maximum(v, 0.0) + jnp.log(1.0 + jnp.exp(-jnp.abs(v))) - log_two)


def leaky_slope(v):
    return 0.55 + 0.45 * jnp.tanh(0.5 * v)


def left_product(left, right):
    return lax.dot_general(
        left, right, (((0,), (0,)), ((), ())), preferred_element_type=jnp.float32
    )


def at_device(group, index):
    return (group, index)


def gather_kernel(n, x_ref, o_ref, send_sem, recv_sem):
    group = lax.axis_index("groups")
    me = lax.axis_index("tm")
    barrier = pltpu.get_barrier_semaphore()

    def greet(i, carry):
        pl.semaphore_signal(
            barrier, inc=1, device_id=at_device(group, (me + i) % n), device_id_type=MESH
        )
        return carry

    lax.fori_loop(1, n, greet, 0)
    pl.semaphore_wait(barrier, n - 1)

    def copy_to(i):
        return pltpu.make_async_remote_copy(
            src_ref=x_ref,
            dst_ref=o_ref.at[me],
            send_sem=send_sem.at[i],
            recv_sem=recv_sem.at[i],
            device_id=at_device(group, (me + i) % n),
            device_id_type=MESH,
        )

    def copy_from(i):
        source = (me + n - i) % n
        return pltpu.make_async_remote_copy(
            src_ref=x_ref,
            dst_ref=o_ref.at[source],
            send_sem=send_sem.at[i],
            recv_sem=recv_sem.at[i],
            device_id=at_device(group, (me + i) % n),
            device_id_type=MESH,
        )

    def send(i, carry):
        copy_to(i).start()
        return carry

    lax.fori_loop(1, n, send, 0)
    o_ref[me] = x_ref[...]

    def finish(i, carry):
        copy_from(i).wait()
        return carry

    lax.fori_loop(1, n, finish, 0)


def gather_all(x, n):
    return pl.pallas_call(
        functools.partial(gather_kernel, n),
        out_shape=jax.ShapeDtypeStruct((n,) + x.shape, x.dtype),
        in_specs=[pl.BlockSpec(memory_space=VMEM)],
        out_specs=pl.BlockSpec(memory_space=VMEM),
        scratch_shapes=[pltpu.SemaphoreType.DMA((n,)), pltpu.SemaphoreType.DMA((n,))],
        compiler_params=pltpu.CompilerParams(collective_id=0, has_side_effects=True),
    )(x)


def stream_plan(nbits, order):
    left = list(range(nbits))[::-1]
    plan = []
    for bit in order:
        place = left.index(bit)
        plan.append((bit, 2**place, 2 ** (len(left) - place - 1)))
        left.remove(bit)
    return plan


def scatter_kernel(n, nbits, plans, targets, *refs):
    count = len(plans)
    ins, refs = refs[:count], refs[count:]
    outs, refs = refs[:2], refs[2:]
    held, refs = refs[: count * (nbits - 1)], refs[count * (nbits - 1) :]
    landed, refs = refs[: count * nbits], refs[count * nbits :]
    send_sem, recv_sem = refs
    group = lax.axis_index("groups")
    me = lax.axis_index("tm")
    bits = [(me // 2**b) % 2 for b in range(nbits)]
    mates = [me + (1 - 2 * bits[b]) * 2**b for b in range(nbits)]
    barrier = pltpu.get_barrier_semaphore()
    for b in range(nbits):
        pl.semaphore_signal(
            barrier, inc=1, device_id=at_device(group, mates[b]), device_id_type=MESH
        )
    pl.semaphore_wait(barrier, nbits)

    def source(s, t):
        return ins[s] if t == 0 else held[s * (nbits - 1) + t - 1]

    def copy(s, t):
        bit = plans[s][t][0]
        return pltpu.make_async_remote_copy(
            src_ref=source(s, t).at[:, 1 - bits[bit]],
            dst_ref=landed[s * nbits + t],
            send_sem=send_sem.at[s * nbits + t],
            recv_sem=recv_sem.at[s * nbits + t],
            device_id=at_device(group, mates[bit]),
            device_id_type=MESH,
        )

    for s in range(count):
        copy(s, 0).start()
    for t in range(nbits):
        for s in range(count):
            copy(s, t).wait_recv()
            bit, hi, lo = plans[s][t]
            here, there = source(s, t), landed[s * nbits + t]
            if t < nbits - 1:
                _, _, next_lo = plans[s][t + 1]
                for i in range(hi * lo):
                    total = here[i // lo, bits[bit], i % lo] + there[i // lo, i % lo]
                    held[s * (nbits - 1) + t][
                        i // (2 * next_lo), (i // next_lo) % 2, i % next_lo
                    ] = total
                copy(s, t + 1).start()
            else:
                which, column, width = targets[s]
                outs[which][:, column : column + width] = here[0, bits[bit], 0] + there[0, 0]
    for t in range(nbits):
        for s in range(count):
            copy(s, t).wait_send()


def scatter_sums(term_pre, terms_up, n):
    nbits = n.bit_length() - 1
    first = tuple(range(nbits))
    second = (0,) + tuple(range(2, nbits)) + (1,)
    arrays = [term_pre] + terms_up
    orders = [first] + [second, first, second, first, second]
    plans = [stream_plan(nbits, order) for order in orders]
    ins, held, landed = [], [], []
    for x, plan in zip(arrays, plans):
        rows, width = x.shape[0] // n, x.shape[1]
        _, hi, lo = plan[0]
        ins.append(x.reshape(hi, 2, lo, rows, width))
        for t, (_, hi, lo) in enumerate(plan):
            if t > 0:
                held.append(VMEM((hi, 2, lo, rows, width), jnp.float32))
            landed.append(VMEM((hi, lo, rows, width), jnp.float32))
    targets = [(0, 0, term_pre.shape[1])] + [(1, C * j, C) for j in range(len(terms_up))]
    sems = len(arrays) * nbits
    return pl.pallas_call(
        functools.partial(scatter_kernel, n, nbits, plans, targets),
        out_shape=[
            jax.ShapeDtypeStruct((term_pre.shape[0] // n, term_pre.shape[1]), jnp.float32),
            jax.ShapeDtypeStruct((terms_up[0].shape[0] // n, C * len(terms_up)), jnp.float32),
        ],
        in_specs=[pl.BlockSpec(memory_space=VMEM)] * len(ins),
        out_specs=[pl.BlockSpec(memory_space=VMEM)] * 2,
        scratch_shapes=held
        + landed
        + [pltpu.SemaphoreType.DMA((sems,)), pltpu.SemaphoreType.DMA((sems,))],
        compiler_params=pltpu.CompilerParams(
            collective_id=1, has_side_effects=True, vmem_limit_bytes=48 << 20
        ),
    )(*ins)


def frame_ids_of(gathered, total_frames):
    n = gathered.shape[0]
    all_ids = gathered[:, 0].reshape(-1)
    dur_rows = gathered[:, 1].reshape(n, -1)
    row_units = dur_rows.shape[1]
    unit_iota = jnp.arange(row_units, dtype=jnp.int32)
    upper = (unit_iota[:, None] <= unit_iota[None, :]).astype(jnp.bfloat16)
    within = jnp.dot(dur_rows.astype(jnp.bfloat16), upper, preferred_element_type=jnp.float32)
    row_total = within[:, row_units - 1]
    offsets = jnp.cumsum(row_total) - row_total
    unit_ends = (within + offsets[:, None]).reshape(-1).astype(jnp.int32)
    width = EXT + 2
    positions = lax.axis_index("tm") * F_DEV - HALO - 1 + jnp.arange(width, dtype=jnp.int32)
    far_end = jnp.full((width,), total_frames + width, jnp.int32)
    ends_padded = jnp.concatenate([unit_ends, far_end])
    ids_padded = jnp.concatenate([all_ids, jnp.zeros((width + 1,), jnp.int32)])
    first_unit = jnp.sum((unit_ends <= positions[0]).astype(jnp.int32))
    window_ends = lax.dynamic_slice_in_dim(ends_padded, first_unit, width)
    window_ids = lax.dynamic_slice_in_dim(ids_padded, first_unit, width + 1)
    local_unit = jnp.sum((window_ends[None, :] <= positions[:, None]).astype(jnp.int32), axis=1)
    slot_iota = jnp.arange(width + 1, dtype=jnp.int32)
    picks = local_unit[:, None] == slot_iota[None, :]
    frame_ids = jnp.sum(jnp.where(picks, window_ids[None, :], 0), axis=1)
    inside = (positions >= 0) & (positions < total_frames)
    frame_ids = jnp.where(inside, frame_ids, -1)
    spare = FRONT * (-(-width // FRONT)) - width
    return jnp.concatenate([frame_ids, jnp.full((spare,), -1, jnp.int32)])[:, None]


def tap_places():
    reads = np.zeros((UP, 5, KD, TURNS * 8), np.float32)
    adds = np.zeros((TURNS * 8, UP * PAIRS), np.float32)
    for phase in range(UP):
        for r, period in enumerate(period_list):
            for k in range(KD):
                ahead = phase + k * period
                reads[phase, r, k, (ahead // UP) * 8 + ahead % UP] = 1.0
                behind = phase - k * period
                row = (-(behind // UP)) * 8 + phase
                adds[row, (behind % UP) * PAIRS + r * KD + k] = 1.0
    return reads, adds


def halves(x):
    high = x.astype(jnp.bfloat16)
    return high, (x - high.astype(jnp.float32)).astype(jnp.bfloat16)


def disc_matrices(disc_taps, disc_out):
    reads, adds = tap_places()
    spread = jnp.sum(disc_taps[None, :, :, :, None] * reads[:, :, :, None, :], axis=2)
    high, low = halves(spread.reshape(UP * CHANNELS, TURNS * 8))
    read_matrix = jnp.concatenate([high, high, low], axis=1)
    own = jnp.asarray(np.eye(5, dtype=np.float32))
    weighted = disc_taps * disc_out[:, None, :]
    repeated = jnp.broadcast_to(disc_out[:, None, :], disc_taps.shape)
    parts = []
    for x in (weighted, repeated):
        full = (x[:, :, None, :] * own[:, None, :, None]).reshape(25, CHANNELS)
        full = jnp.concatenate([full, jnp.zeros((PAIRS - 25, CHANNELS), jnp.float32)], axis=0)
        parts.append(jnp.concatenate(halves(full), axis=0))
    add_matrix = jnp.asarray(np.concatenate([adds, adds], axis=1), jnp.bfloat16)
    return read_matrix, parts[0], parts[1], add_matrix


def split_dot(matrix, x):
    high, low = halves(x)
    both = jnp.dot(matrix, high, preferred_element_type=jnp.float32)
    rest = jnp.dot(matrix[:PAIRS], low, preferred_element_type=jnp.float32)
    return both[:PAIRS] + both[PAIRS:] + rest


def step_kernel(
    total_frames,
    ids_ref,
    table_ref,
    pre_w,
    up_w,
    post_ref,
    read_ref,
    weighted_ref,
    repeated_ref,
    add_ref,
    window_o,
    act_o,
    up_grad_o,
    pre_grad_o,
    wave_o,
    wave_grad_o,
    rows,
    window,
    pre_out,
    pre_act,
    up_out,
    columns,
    wave,
    shifted,
    sums,
):
    first_frame = lax.axis_index("tm") * F_DEV - HALO
    vocab = table_ref.shape[0]

    def embed(i, carry):
        at = pl.multiple_of(i * FRONT, FRONT)
        ids = ids_ref[pl.ds(at, FRONT), :]
        one_hot = (ids == lax.broadcasted_iota(jnp.int32, (FRONT, vocab), 1)).astype(jnp.bfloat16)
        rows[pl.ds(at, FRONT), :] = jnp.dot(
            one_hot, table_ref[...], preferred_element_type=jnp.float32
        )
        return carry

    lax.fori_loop(0, ids_ref.shape[0] // FRONT, embed, 0)

    columns[pl.ds(EXT, LANES - EXT), :] = jnp.zeros((LANES - EXT, 128), jnp.float32)
    lane = lax.broadcasted_iota(jnp.int32, (FRONT, 128), 1)
    for i in range(EXT // FRONT):
        at = i * FRONT
        taps = [rows[at + k : at + k + FRONT, :].astype(jnp.bfloat16) for k in range(3)]
        win = jnp.concatenate(taps, axis=1)
        window[at : at + FRONT, :] = win
        pre = jnp.dot(win, pre_w[...], preferred_element_type=jnp.float32).astype(jnp.bfloat16)
        pre_out[at : at + FRONT, :] = pre
        act = leaky_relu(pre.astype(jnp.float32)).astype(jnp.bfloat16)
        pre_act[at : at + FRONT, :] = act
        column = jnp.zeros((FRONT, 128), jnp.float32)
        for j in range(UP):
            up = jnp.dot(
                act, up_w[:, C * j : C * (j + 1)], preferred_element_type=jnp.float32
            ).astype(jnp.bfloat16)
            up_out[at : at + FRONT, C * j : C * (j + 1)] = up
            terms = leaky_relu(up.astype(jnp.float32)) * post_ref[...]
            column = jnp.where(lane == j, jnp.sum(terms, axis=1, keepdims=True), column)
        columns[at : at + FRONT, :] = column

    frame = lax.broadcasted_iota(jnp.int32, (8, LANES), 1) + first_frame
    for b in range(LANES // 128):
        at = 128 * b
        wave[:, at : at + 128] = columns[at : at + 128, :].T[:8, :]
    inside = (frame >= 0) & (frame < total_frames)
    signal = jnp.where(inside, jnp.tanh(wave[...]), 0.0)
    wave[...] = signal
    depth = TURNS * 8
    for q in range(0, TURNS, 2):
        turned = [signal if t == 0 else pltpu.roll(signal, LANES - t, 1) for t in (q, q + 1)]
        high, low = halves(jnp.concatenate(turned, axis=0))
        shifted[8 * q : 8 * q + 16, :] = high
        shifted[depth + 8 * q : depth + 8 * q + 16, :] = low
        shifted[2 * depth + 8 * q : 2 * depth + 8 * q + 16, :] = high

    chunk_lane = lax.broadcasted_iota(jnp.int32, (PAIRS, CHUNK), 1)

    def judge(i, carry):
        at = pl.multiple_of(i * CHUNK, CHUNK)
        real = chunk_lane + (at + first_frame) >= 0
        taps = shifted[:, pl.ds(at, CHUNK)]
        highs, lows = [], []
        for j in range(UP):
            pre = jnp.dot(
                read_ref[CHANNELS * j : CHANNELS * (j + 1), :],
                taps,
                preferred_element_type=jnp.float32,
            )
            scores = split_dot(repeated_ref[...], leaky_relu(pre))
            adjoint = split_dot(weighted_ref[...], leaky_slope(pre)) * (scores - 1.0)
            high, low = halves(jnp.where(real, adjoint, 0.0))
            highs.append(high)
            lows.append(low)
        sums[:, pl.ds(at, CHUNK)] = jnp.dot(
            add_ref[...], jnp.concatenate(highs + lows, axis=0), preferred_element_type=jnp.float32
        )
        return carry

    lax.fori_loop(0, LANES // CHUNK, judge, 0)
    wave_grad = sums[0:8, :]
    for q in range(1, TURNS):
        wave_grad = wave_grad + pltpu.roll(sums[8 * q : 8 * q + 8, :], q, 1)
    wave_o[...] = signal
    wave_grad_o[...] = wave_grad
    sums[0:8, :] = wave_grad * (1.0 - signal * signal)
    for b in range(LANES // 128):
        at = 128 * b
        columns[at : at + 128, 0:8] = sums[0:8, at : at + 128].T

    for i in range(F_DEV // BACK):
        to, at = i * BACK, i * BACK + HALO
        window_o[to : to + BACK, :] = window[at : at + BACK, :]
        act_o[to : to + BACK, :] = pre_act[at : at + BACK, :]
        hidden = jnp.zeros((BACK, up_w.shape[0]), jnp.float32)
        for j in range(UP):
            slope = leaky_slope(up_out[at : at + BACK, C * j : C * (j + 1)].astype(jnp.float32))
            grad = columns[at : at + BACK, j : j + 1] * post_ref[...] * slope
            grad = grad.astype(jnp.bfloat16)
            up_grad_o[to : to + BACK, C * j : C * (j + 1)] = grad
            hidden = hidden + lax.dot_general(
                grad,
                up_w[:, C * j : C * (j + 1)],
                (((1,), (1,)), ((), ())),
                preferred_element_type=jnp.float32,
            )
        slope = leaky_slope(pre_out[at : at + BACK, :].astype(jnp.float32))
        pre_grad_o[to : to + BACK, :] = (hidden * slope).astype(jnp.bfloat16)


def step(frame_ids, unit_table, pre_weight, up_weight, post_weight, matrices, total_frames):
    width, depth = up_weight.shape[1], up_weight.shape[0]
    shape, bf16, f32 = jax.ShapeDtypeStruct, jnp.bfloat16, jnp.float32
    operands = (frame_ids, unit_table, pre_weight, up_weight, post_weight[None, :], *matrices)
    return pl.pallas_call(
        functools.partial(step_kernel, total_frames),
        out_shape=[
            shape((F_DEV, pre_weight.shape[0]), bf16),
            shape((F_DEV, depth), bf16),
            shape((F_DEV, width), bf16),
            shape((F_DEV, depth), bf16),
            shape((8, LANES), f32),
            shape((8, LANES), f32),
        ],
        in_specs=[pl.BlockSpec(memory_space=VMEM)] * len(operands),
        out_specs=[pl.BlockSpec(memory_space=VMEM)] * 6,
        scratch_shapes=[
            VMEM((frame_ids.shape[0], unit_table.shape[1]), f32),
            VMEM((EXT, pre_weight.shape[0]), bf16),
            VMEM((EXT, depth), bf16),
            VMEM((EXT, depth), bf16),
            VMEM((EXT, width), bf16),
            VMEM((LANES, 128), f32),
            VMEM((8, LANES), f32),
            VMEM((3 * TURNS * 8, LANES), bf16),
            VMEM((TURNS * 8, LANES), f32),
        ],
        compiler_params=pltpu.CompilerParams(vmem_limit_bytes=50 << 20),
    )(*operands)


def per_device(
    unit_ids, durations, unit_table, pre_weight, up_weight, post_weight, disc_taps, disc_out
):
    devices = lax.axis_size("tm")
    total_frames = F_DEV * devices
    total_samples = UP * total_frames
    matrices = disc_matrices(disc_taps, disc_out)
    gathered = gather_all(jnp.stack([unit_ids.reshape(-1, 128), durations.reshape(-1, 128)]), devices)
    frame_ids = frame_ids_of(gathered, total_frames)
    frame_window, act, up_grad, pre_grad, wave, wave_grad = step(
        frame_ids, unit_table, pre_weight, up_weight, post_weight, matrices, total_frames
    )
    terms_up = [left_product(act, up_grad[:, C * j : C * (j + 1)]) for j in range(UP)]
    term_pre = left_product(frame_window, pre_grad)
    grad_pre, grad_up = scatter_sums(term_pre, terms_up, devices)
    mean_scale = 1.0 / total_samples
    both = jnp.stack([wave, wave_grad])[:, :UP, HALO : HALO + F_DEV]
    both = both.transpose(0, 2, 1).reshape(2, -1)
    return (both[0], both[1], grad_pre * mean_scale, grad_up * mean_scale)


def solution(mesh):
    in_specs = (P(("groups", "tm")), P(("groups", "tm")), P(), P(), P(), P(), P(), P())
    out_specs = (
        P(("groups", "tm")),
        P(("groups", "tm")),
        P(("groups", "tm"), None),
        P(("groups", "tm"), None),
    )
    return jax.shard_map(
        per_device, mesh=mesh, in_specs=in_specs, out_specs=out_specs, check_vma=False
    )
```

profile of v0, /device:TPU:0, one launch (start us, length us, event | category | flops | bytes accessed | tf_op | source)
XLA Modules:
  0.0 101.4 jit_solution(11749679540088619332)
XLA Ops:
  0.7 0.5 slice.53
  1.2 1.3 %pad_add_fusion.x_ref = s32[2,6,128]{2,1,0:T(8,128)} fusion(s32[1,6,128]{2,1,0:T(8,128)} %bitcast.42, s32[1,6,128]{2,1,0:T(8,128)} %bitcast.43), kind=kLoop, calls=%fused_computation.40 | loop fusion | flops 1536 | bytes 12288 | tf_op jit(solution)/shard_map/stack | solution.py:450
  2.5 10.3 %shard_map.138 = s32[16,2,6,128]{3,2,1,0:T(8,128)} custom-call(s32[2,6,128]{2,1,0:T(8,128)} %pad_add_fusion.x_ref), custom_call_target="tpu_custom_call" | custom-call | tf_op jit(solution)/shard_map/pallas_call | solution.py:99
  12.8 0.9 fusion.15
  13.7 0.2 fusion
  14.0 0.2 subtract_reduce_fusion
  14.2 1.4 %convert_reduce_fusion.1 = (s32[]{:T(128)}, s32[16,768]{1,0:T(8,128)S(1)}) fusion(s32[]{:T(128)} %bitcast.2, f32[16,768]{1,0:T(8,128)S(1)} %fusion, f32[16]{0:T(128)S(1)} %subtract_reduce_fusion), kind=kLoop, calls=%fused_computation.28 | loop fusion | flops 61439 | bytes 98376 | tf_op jit(solution)/shard_map/reduce_sum | solution.py:225
  17.6 0.1 pad_dynamic-slice_fusion
  19.0 0.1 pad_dynamic-slice_fusion.1
  19.1 1.2 %convert_reduce_fusion = s32[1570]{0:T(1024)S(1)} fusion(s32[1570]{0:T(1024)S(1)} %pad_dynamic-slice_fusion.1, s32[1570]{0:T(1024)S(1)} %iota_add_fusion), kind=kLoop, calls=%fused_computation.2 | loop fusion | flops 7393130 | bytes 18840 | tf_op jit(solution)/shard_map/reduce_sum | solution.py:228
  20.3 1.7 %select_reduce_fusion = s32[1570]{0:T(1024)S(1)} fusion(s32[1571]{0:T(1024)S(1)} %pad_dynamic-slice_fusion, s32[1570]{0:T(1024)S(1)} %convert_reduce_fusion), kind=kLoop, calls=%fused_computation | loop fusion | flops 7397840 | bytes 18844 | tf_op jit(solution)/shard_map/reduce_sum | solution.py:231
  22.0 0.3 broadcast_in_dim.20.ids_ref
  22.3 0.3 multiply_reduce_fusion
  22.6 0.3 pad_maximum_fusion.read_ref
  22.9 0.1 broadcast_multiply_fusion.1
  23.0 0.1 mul.75
  23.2 0.1 mul.77
  23.3 35.4 %shard_map.139 = (bf16[1536,384]{1,0:T(8,128)(2,1)S(1)}, bf16[1536,512]{1,0:T(8,128)(2,1)}, bf16[1536,1280]{1,0:T(8,128)(2,1)}, bf16[1536,512]{1,0:T(8,128)(2,1)...) custom-call(s32[1792,1]{1,0:T(8,128)S(1)} %broadcast_in_dim.20.ids_ref, bf16[1000,128]{1,0:T(8,128)(2,1)S(1)} %copy-done.1, ...), custom_call_target="tpu_custom_call" | custom-call | tf_op jit(solution)/shard_map/pallas_call | solution.py:416
  58.9 0.3 copy.19
  59.2 1.2 %squeeze.11 = f32[7680]{0:T(1024)} reshape(f32[1,1536,5]{2,1,0:T(8,128)S(1)} %copy.19) | data formatting | bytes 61440 | tf_op jit(solution)/shard_map/squeeze | solution.py:461
  60.4 0.3 copy.20
  60.6 1.2 %squeeze.12 = f32[7680]{0:T(1024)} reshape(f32[1,1536,5]{2,1,0:T(8,128)S(1)} %copy.20) | data formatting | bytes 61440 | tf_op jit(solution)/shard_map/squeeze | solution.py:461
  61.8 2.3 %fusion.17 = f32[384,512]{1,0:T(8,128)S(1)} fusion(bf16[1536,384]{1,0:T(8,128)(2,1)S(1)} %get-tuple-element.14, bf16[1536,512]{1,0:T(8,128)(2,1)} %get-tuple-element.15), kind=kOutput, calls=%fused_computation.46 | convolution fusion | flops 603979776 | bytes 3538944 | tf_op jit(solution)/shard_map/dot_general | solution.py:40
  64.2 1.9 %fusion.9 = f32[512,256]{1,0:T(8,128)S(1)} fusion(bf16[1536,512]{1,0:T(8,128)(2,1)S(1)} %copy-done.9, bf16[1536,1280]{1,0:T(8,128)(2,1)} %get-tuple-element.17), kind=kOutput, calls=%fused_computation.14 | convolution fusion | flops 402653184 | bytes 2883584 | tf_op jit(solution)/shard_map/dot_general | solution.py:40
  66.1 0.5 copy-done.8
  66.5 0.6 fusion.7
  67.1 0.6 fusion.5
  67.8 0.6 fusion.3
  68.4 0.6 fusion.1
  69.0 31.1 %shard_map.140 = (f32[24,512]{1,0:T(8,128)S(1)}, f32[32,1280]{1,0:T(8,128)S(1)}) custom-call(f32[8,2,1,24,512]{4,3,2,1,0:T(8,128)S(1)} %bitcast.32, f32[8,2,1,32,256]{4,3,2,1,0:T(8,128)S(1)} %bitcast.33, f32[8,2,1,32,256]{4,3,2,1,0:T(8,128)S(1)} %bitcast.34, f32[8,2,1,32,256]{4,3,2,1,0:T(8,128)S(1)} %bitcast.35, f32[8,2,1,32,256]{4,3,2,1,0:T(8,128)S(1)} %bitcast.36, ...), custom_call_target="tpu_custom_call" | custom-call | tf_op jit(solution)/shard_map/pallas_call | solution.py:192
  100.1 0.6 broadcast_multiply_fusion.3
  100.7 0.7 broadcast_multiply_fusion
  (35 shorter events, 0.4 us)
Async XLA Ops:
  0.6 21.6 %copy-start.4 = (f32[5,5,5,80]{3,2,1,0:T(8,128)S(1)}, f32[5,5,5,80]{3,2,1,0:T(8,128)}, u32[]{:S(2)}) copy-start(f32[5,5,5,80]{3,2,1,0:T(8,128)} %constant.55) | copy-start | bytes 120004
  0.6 21.6 %copy-start.5 = (f32[5,5,32]{2,1,0:T(8,128)S(1)}, f32[5,5,32]{2,1,0:T(8,128)}, u32[]{:S(2)}) copy-start(f32[5,5,32]{2,1,0:T(8,128)} %param.17) | copy-start | bytes 9604
  13.7 9.2 %copy-start.6 = (f32[5,32]{1,0:T(8,128)S(1)}, f32[5,32]{1,0:T(8,128)}, u32[]{:S(2)}) copy-start(f32[5,32]{1,0:T(8,128)} %param.18) | copy-start | bytes 1924
  13.7 9.2 %copy-start.7 = (f32[5,5]{1,0:T(8,128)S(1)}, f32[5,5]{1,0:T(8,128)}, u32[]{:S(2)}) copy-start(f32[5,5]{1,0:T(8,128)} %constant.13.clone) | copy-start | bytes 304
  19.0 4.2 %copy-start = (bf16[384,512]{1,0:T(8,128)(2,1)S(1)}, bf16[384,512]{1,0:T(8,128)(2,1)}, u32[]{:S(2)}) copy-start(bf16[384,512]{1,0:T(8,128)(2,1)} %pre_w.1) | copy-start | bytes 1179652
  19.0 4.3 %copy-start.1 = (bf16[1000,128]{1,0:T(8,128)(2,1)S(1)}, bf16[1000,128]{1,0:T(8,128)(2,1)}, u32[]{:S(2)}) copy-start(bf16[1000,128]{1,0:T(8,128)(2,1)} %table_ref.1) | copy-start | bytes 768004
  19.1 4.3 %copy-start.2 = (bf16[80,320]{1,0:T(8,128)(2,1)S(1)}, bf16[80,320]{1,0:T(8,128)(2,1)}, u32[]{:S(2)}) copy-start(bf16[80,320]{1,0:T(8,128)(2,1)} %constant.44.clone.add_ref) | copy-start | bytes 153604
  19.1 4.3 %copy-start.3 = (f32[256]{0:T(256)S(1)}, f32[256]{0:T(256)}, u32[]{:S(2)}) copy-start(f32[256]{0:T(256)} %param.16) | copy-start | bytes 3076
  61.8 2.3 %copy-start.9 = (bf16[1536,512]{1,0:T(8,128)(2,1)S(1)}, bf16[1536,512]{1,0:T(8,128)(2,1)}, u32[]{:S(2)}) copy-start(bf16[1536,512]{1,0:T(8,128)(2,1)} %get-tuple-element.16) | copy-start | bytes 4718596
  64.2 2.4 %copy-start.8 = (bf16[1536,1280]{1,0:T(8,128)(2,1)S(1)}, bf16[1536,1280]{1,0:T(8,128)(2,1)}, u32[]{:S(2)}) copy-start(bf16[1536,1280]{1,0:T(8,128)(2,1)} %get-tuple-element.17) | copy-start | bytes 11796484
where the time goes:
time: 102 us; the launch traced here: 101 us
  Pallas kernels  76.8 us (75%)
  other arithmetic  8.8 us (9%)
  matrix products  6.86 us (7%)
  local copies, waits for them, and re-layouts  4.7 us (5%)
  between operations  4.2 us (4%)
    pallas_call x1, Pallas kernels, step(): pl.pallas_call(functools.partial(step_kernel, total_frames), out_shape=[s...  35.4 us
    pallas_call x1, Pallas kernels, scatter_sums(): pl.pallas_call(functools.partial(scatter_kernel, n, nbits, plans, targets...  31.1 us
    pallas_call x1, Pallas kernels, gather_all(): pl.pallas_call(functools.partial(gather_kernel, n), out_shape=jax.ShapeDt...  10.3 us
    dot_general x6, matrix products, left_product(): lax.dot_general(left, right, (((0,), (0,)), ((), ())), preferred_element_...  6.65 us
    squeeze x2, local copies, waits for them, and re-layouts, per_device(): return (both[0], both[1], grad_pre * mean_scale, grad_up * mean_scale)  2.35 us

commit v1 on v0

--- a/solution.py
+++ b/solution.py
@@ -36,12 +36,6 @@
     return 0.55 + 0.45 * jnp.tanh(0.5 * v)
 
 
-def left_product(left, right):
-    return lax.dot_general(
-        left, right, (((0,), (0,)), ((), ())), preferred_element_type=jnp.float32
-    )
-
-
 def at_device(group, index):
     return (group, index)
 
@@ -116,94 +110,73 @@
     return plan
 
 
-def scatter_kernel(n, nbits, plans, targets, *refs):
-    count = len(plans)
-    ins, refs = refs[:count], refs[count:]
-    outs, refs = refs[:2], refs[2:]
-    held, refs = refs[: count * (nbits - 1)], refs[count * (nbits - 1) :]
-    landed, refs = refs[: count * nbits], refs[count * nbits :]
-    send_sem, recv_sem = refs
-    group = lax.axis_index("groups")
-    me = lax.axis_index("tm")
-    bits = [(me // 2**b) % 2 for b in range(nbits)]
-    mates = [me + (1 - 2 * bits[b]) * 2**b for b in range(nbits)]
-    barrier = pltpu.get_barrier_semaphore()
-    for b in range(nbits):
-        pl.semaphore_signal(
-            barrier, inc=1, device_id=at_device(group, mates[b]), device_id_type=MESH
-        )
-    pl.semaphore_wait(barrier, nbits)
-
-    def source(s, t):
-        return ins[s] if t == 0 else held[s * (nbits - 1) + t - 1]
-
-    def copy(s, t):
-        bit = plans[s][t][0]
-        return pltpu.make_async_remote_copy(
-            src_ref=source(s, t).at[:, 1 - bits[bit]],
-            dst_ref=landed[s * nbits + t],
-            send_sem=send_sem.at[s * nbits + t],
-            recv_sem=recv_sem.at[s * nbits + t],
-            device_id=at_device(group, mates[bit]),
-            device_id_type=MESH,
-        )
-
-    for s in range(count):
-        copy(s, 0).start()
-    for t in range(nbits):
-        for s in range(count):
-            copy(s, t).wait_recv()
-            bit, hi, lo = plans[s][t]
-            here, there = source(s, t), landed[s * nbits + t]
-            if t < nbits - 1:
-                _, _, next_lo = plans[s][t + 1]
-                for i in range(hi * lo):
-                    total = here[i // lo, bits[bit], i % lo] + there[i // lo, i % lo]
-                    held[s * (nbits - 1) + t][
-                        i // (2 * next_lo), (i // next_lo) % 2, i % next_lo
-                    ] = total
-                copy(s, t + 1).start()
-            else:
-                which, column, width = targets[s]
-                outs[which][:, column : column + width] = here[0, bits[bit], 0] + there[0, 0]
-    for t in range(nbits):
-        for s in range(count):
-            copy(s, t).wait_send()
-
-
-def scatter_sums(term_pre, terms_up, n):
+def stream_plans(n):
     nbits = n.bit_length() - 1
     first = tuple(range(nbits))
     second = (0,) + tuple(range(2, nbits)) + (1,)
-    arrays = [term_pre] + terms_up
-    orders = [first] + [second, first, second, first, second]
-    plans = [stream_plan(nbits, order) for order in orders]
-    ins, held, landed = [], [], []
-    for x, plan in zip(arrays, plans):
-        rows, width = x.shape[0] // n, x.shape[1]
-        _, hi, lo = plan[0]
-        ins.append(x.reshape(hi, 2, lo, rows, width))
-        for t, (_, hi, lo) in enumerate(plan):
-            if t > 0:
-                held.append(VMEM((hi, 2, lo, rows, width), jnp.float32))
-            landed.append(VMEM((hi, lo, rows, width), jnp.float32))
-    targets = [(0, 0, term_pre.shape[1])] + [(1, C * j, C) for j in range(len(terms_up))]
-    sems = len(arrays) * nbits
-    return pl.pallas_call(
-        functools.partial(scatter_kernel, n, nbits, plans, targets),
-        out_shape=[
-            jax.ShapeDtypeStruct((term_pre.shape[0] // n, term_pre.shape[1]), jnp.float32),
-            jax.ShapeDtypeStruct((terms_up[0].shape[0] // n, C * len(terms_up)), jnp.float32),
-        ],
-        in_specs=[pl.BlockSpec(memory_space=VMEM)] * len(ins),
-        out_specs=[pl.BlockSpec(memory_space=VMEM)] * 2,
-        scratch_shapes=held
-        + landed
-        + [pltpu.SemaphoreType.DMA((sems,)), pltpu.SemaphoreType.DMA((sems,))],
-        compiler_params=pltpu.CompilerParams(
-            collective_id=1, has_side_effects=True, vmem_limit_bytes=48 << 20
-        ),
-    )(*ins)
+    orders = [second, first, second, first, second, first, second]
+    return nbits, [stream_plan(nbits, order) for order in orders]
+
+
+class Halving:
+    def __init__(self, n, outs, targets, terms, held, landed, send_sem, recv_sem):
+        self.nbits, self.plans = stream_plans(n)
+        self.outs, self.targets, self.terms = outs, targets, terms
+        self.held, self.landed = held, landed
+        self.send_sem, self.recv_sem = send_sem, recv_sem
+        self.group, me = lax.axis_index("groups"), lax.axis_index("tm")
+        self.bits = [(me // 2**b) % 2 for b in range(self.nbits)]
+        self.mates = [me + (1 - 2 * self.bits[b]) * 2**b for b in range(self.nbits)]
+
+    def greet(self):
+        barrier = pltpu.get_barrier_semaphore()
+        for mate in self.mates:
+            pl.semaphore_signal(
+                barrier, inc=1, device_id=at_device(self.group, mate), device_id_type=MESH
+            )
+
+    def meet(self):
+        pl.semaphore_wait(pltpu.get_barrier_semaphore(), self.nbits)
+
+    def source(self, s, t):
+        return self.terms[s] if t == 0 else self.held[s * (self.nbits - 1) + t - 1]
+
+    def copy(self, s, t):
+        bit = self.plans[s][t][0]
+        return pltpu.make_async_remote_copy(
+            src_ref=self.source(s, t).at[:, 1 - self.bits[bit]],
+            dst_ref=self.landed[s * self.nbits + t],
+            send_sem=self.send_sem.at[s * self.nbits + t],
+            recv_sem=self.recv_sem.at[s * self.nbits + t],
+            device_id=at_device(self.group, self.mates[bit]),
+            device_id_type=MESH,
+        )
+
+    def put(self, s, term):
+        ref = self.terms[s]
+        ref[...] = term.reshape(ref.shape)
+        self.copy(s, 0).start()
+
+    def advance(self, s, t):
+        self.copy(s, t).wait_recv()
+        bit, hi, lo = self.plans[s][t]
+        mine = self.bits[bit]
+        here, there = self.source(s, t), self.landed[s * self.nbits + t]
+        if t == self.nbits - 1:
+            which, column = self.targets[s]
+            self.outs[which][:, column : column + C] = here[0, mine, 0] + there[0, 0]
+            return
+        _, _, next_lo = self.plans[s][t + 1]
+        onward = self.held[s * (self.nbits - 1) + t]
+        for i in range(hi * lo):
+            total = here[i // lo, mine, i % lo] + there[i // lo, i % lo]
+            onward[i // (2 * next_lo), (i // next_lo) % 2, i % next_lo] = total
+        self.copy(s, t + 1).start()
+
+    def finish(self):
+        for t in range(self.nbits):
+            for s in range(len(self.plans)):
+                self.copy(s, t).wait_send()
 
 
 def frame_ids_of(gathered, total_frames):
@@ -279,7 +252,7 @@
 
 
 def step_kernel(
-    total_frames,
+    devices,
     ids_ref,
     table_ref,
     pre_w,
@@ -289,12 +262,10 @@
     weighted_ref,
     repeated_ref,
     add_ref,
-    window_o,
-    act_o,
-    up_grad_o,
-    pre_grad_o,
     wave_o,
     wave_grad_o,
+    grad_pre_o,
+    grad_up_o,
     rows,
     window,
     pre_out,
@@ -304,7 +275,21 @@
     wave,
     shifted,
     sums,
+    up_grad,
+    pre_grad,
+    window_t,
+    act_t,
+    *stream_refs,
 ):
+    nbits, plans = stream_plans(devices)
+    count = len(plans)
+    terms, stream_refs = stream_refs[:count], stream_refs[count:]
+    held, stream_refs = stream_refs[: count * (nbits - 1)], stream_refs[count * (nbits - 1) :]
+    landed, sems = stream_refs[: count * nbits], stream_refs[count * nbits :]
+    targets = [(1, C * j) for j in range(UP)] + [(0, 0), (0, C)]
+    halving = Halving(devices, (grad_pre_o, grad_up_o), targets, terms, held, landed, *sems)
+    halving.greet()
+    total_frames = devices * F_DEV
     first_frame = lax.axis_index("tm") * F_DEV - HALO
     vocab = table_ref.shape[0]
 
@@ -389,45 +374,69 @@
         at = 128 * b
         columns[at : at + 128, 0:8] = sums[0:8, at : at + 128].T
 
-    for i in range(F_DEV // BACK):
-        to, at = i * BACK, i * BACK + HALO
-        window_o[to : to + BACK, :] = window[at : at + BACK, :]
-        act_o[to : to + BACK, :] = pre_act[at : at + BACK, :]
-        hidden = jnp.zeros((BACK, up_w.shape[0]), jnp.float32)
-        for j in range(UP):
+    blocks = [(i * BACK, i * BACK + HALO) for i in range(F_DEV // BACK)]
+    for to, at in blocks:
+        act_t[:, to : to + BACK] = pre_act[at : at + BACK, :].T
+        window_t[:, to : to + BACK] = window[at : at + BACK, :].T
+    halving.meet()
+    for j in range(UP):
+        for to, at in blocks:
             slope = leaky_slope(up_out[at : at + BACK, C * j : C * (j + 1)].astype(jnp.float32))
             grad = columns[at : at + BACK, j : j + 1] * post_ref[...] * slope
-            grad = grad.astype(jnp.bfloat16)
-            up_grad_o[to : to + BACK, C * j : C * (j + 1)] = grad
-            hidden = hidden + lax.dot_general(
-                grad,
-                up_w[:, C * j : C * (j + 1)],
-                (((1,), (1,)), ((), ())),
-                preferred_element_type=jnp.float32,
-            )
+            up_grad[to : to + BACK, C * j : C * (j + 1)] = grad.astype(jnp.bfloat16)
+        term = jnp.dot(
+            act_t[...], up_grad[:, C * j : C * (j + 1)], preferred_element_type=jnp.float32
+        )
+        halving.put(j, term)
+        if j > 0:
+            halving.advance(j - 1, 0)
+    for to, at in blocks:
+        hidden = lax.dot_general(
+            up_grad[to : to + BACK, :],
+            up_w[...],
+            (((1,), (1,)), ((), ())),
+            preferred_element_type=jnp.float32,
+        )
         slope = leaky_slope(pre_out[at : at + BACK, :].astype(jnp.float32))
-        pre_grad_o[to : to + BACK, :] = (hidden * slope).astype(jnp.bfloat16)
-
-
-def step(frame_ids, unit_table, pre_weight, up_weight, post_weight, matrices, total_frames):
-    width, depth = up_weight.shape[1], up_weight.shape[0]
+        pre_grad[to : to + BACK, :] = (hidden * slope).astype(jnp.bfloat16)
+    halving.advance(UP - 1, 0)
+    for j in range(2):
+        term = jnp.dot(
+            window_t[...], pre_grad[:, C * j : C * (j + 1)], preferred_element_type=jnp.float32
+        )
+        halving.put(UP + j, term)
+    halving.advance(UP, 0)
+    halving.advance(UP + 1, 0)
+    for t in range(1, nbits):
+        for s in range(count):
+            halving.advance(s, t)
+    halving.finish()
+
+
+def step(frame_ids, unit_table, pre_weight, up_weight, post_weight, matrices, devices):
+    width, depth, span = up_weight.shape[1], up_weight.shape[0], pre_weight.shape[0]
     shape, bf16, f32 = jax.ShapeDtypeStruct, jnp.bfloat16, jnp.float32
     operands = (frame_ids, unit_table, pre_weight, up_weight, post_weight[None, :], *matrices)
+    nbits, plans = stream_plans(devices)
+    terms, held, landed = [], [], []
+    for s, plan in enumerate(plans):
+        rows = (depth if s < UP else span) // devices
+        for t, (_, hi, lo) in enumerate(plan):
+            (held if t > 0 else terms).append(VMEM((hi, 2, lo, rows, C), f32))
+            landed.append(VMEM((hi, lo, rows, C), f32))
     return pl.pallas_call(
-        functools.partial(step_kernel, total_frames),
+        functools.partial(step_kernel, devices),
         out_shape=[
-            shape((F_DEV, pre_weight.shape[0]), bf16),
-            shape((F_DEV, depth), bf16),
-            shape((F_DEV, width), bf16),
-            shape((F_DEV, depth), bf16),
             shape((8, LANES), f32),
             shape((8, LANES), f32),
+            shape((span // devices, depth), f32),
+            shape((depth // devices, width), f32),
         ],
         in_specs=[pl.BlockSpec(memory_space=VMEM)] * len(operands),
-        out_specs=[pl.BlockSpec(memory_space=VMEM)] * 6,
+        out_specs=[pl.BlockSpec(memory_space=VMEM)] * 4,
         scratch_shapes=[
             VMEM((frame_ids.shape[0], unit_table.shape[1]), f32),
-            VMEM((EXT, pre_weight.shape[0]), bf16),
+            VMEM((EXT, span), bf16),
             VMEM((EXT, depth), bf16),
             VMEM((EXT, depth), bf16),
             VMEM((EXT, width), bf16),
@@ -435,8 +444,19 @@
             VMEM((8, LANES), f32),
             VMEM((3 * TURNS * 8, LANES), bf16),
             VMEM((TURNS * 8, LANES), f32),
+            VMEM((F_DEV, width), bf16),
+            VMEM((F_DEV, depth), bf16),
+            VMEM((span, F_DEV), bf16),
+            VMEM((depth, F_DEV), bf16),
+            *terms,
+            *held,
+            *landed,
+            pltpu.SemaphoreType.DMA((len(plans) * nbits,)),
+            pltpu.SemaphoreType.DMA((len(plans) * nbits,)),
         ],
-        compiler_params=pltpu.CompilerParams(vmem_limit_bytes=50 << 20),
+        compiler_params=pltpu.CompilerParams(
+            collective_id=1, has_side_effects=True, vmem_limit_bytes=56 << 20
+        ),
     )(*operands)
 
 
@@ -449,12 +469,9 @@
     matrices = disc_matrices(disc_taps, disc_out)
     gathered = gather_all(jnp.stack([unit_ids.reshape(-1, 128), durations.reshape(-1, 128)]), devices)
     frame_ids = frame_ids_of(gathered, total_frames)
-    frame_window, act, up_grad, pre_grad, wave, wave_grad = step(
-        frame_ids, unit_table, pre_weight, up_weight, post_weight, matrices, total_frames
+    wave, wave_grad, grad_pre, grad_up = step(
+        frame_ids, unit_table, pre_weight, up_weight, post_weight, matrices, devices
     )
-    terms_up = [left_product(act, up_grad[:, C * j : C * (j + 1)]) for j in range(UP)]
-    term_pre = left_product(frame_window, pre_grad)
-    grad_pre, grad_up = scatter_sums(term_pre, terms_up, devices)
     mean_scale = 1.0 / total_samples
     both = jnp.stack([wave, wave_grad])[:, :UP, HALO : HALO + F_DEV]
     both = both.transpose(0, 2, 1).reshape(2, -1)

time: 102 us -> 95.7 us (0.938)
  matrix products: 6.86 us -> 0.21 us
  other arithmetic: 8.8 us -> 13.5 us
  Pallas kernels: 76.8 us -> 72.4 us
    dot_general x6 -> x0, matrix products: 6.65 us -> none  [left_product(): lax.dot_general(left, right, (((0,), (0,)), ((), ())), preferred_element_...]
    pallas_call x2 -> x1, Pallas kernels: 66.5 us -> 62.1 us  [step(): pl.pallas_call(functools.partial(step_kernel, devices), out_shape=[shape(...]
    mul x2, other arithmetic: 1.31 us -> 3.02 us  [per_device(): return (both[0], both[1], grad_pre * mean_scale, grad_up * mean_scale)]
where the time goes in v1:
time: 95.7 us; the launch traced here: 95.2 us
  Pallas kernels  72.4 us (76%)
  other arithmetic  13.5 us (14%)
  local copies, waits for them, and re-layouts  5.16 us (5%)
  between operations  4.06 us (4%)
    pallas_call x1, Pallas kernels, step(): pl.pallas_call(functools.partial(step_kernel, devices), out_shape=[shape(...  62.1 us
    pallas_call x1, Pallas kernels, gather_all(): pl.pallas_call(functools.partial(gather_kernel, n), out_shape=jax.ShapeDt...  10.3 us
    mul x2, other arithmetic, per_device(): return (both[0], both[1], grad_pre * mean_scale, grad_up * mean_scale)  3.02 us
    squeeze x2, local copies, waits for them, and re-layouts, per_device(): return (both[0], both[1], grad_pre * mean_scale, grad_up * mean_scale)  2.35 us

profile of v1, /device:TPU:0, one launch (start us, length us, event | category | flops | bytes accessed | tf_op | source)
XLA Modules:
  0.0 95.2 jit_solution(8469440618559192392)
XLA Ops:
  0.6 0.0 copy-start.3
  0.6 0.0 copy-start
  0.7 0.0 copy-start.2
  0.7 0.5 slice.33
  1.2 1.3 %pad_add_fusion.x_ref = s32[2,6,128]{2,1,0:T(8,128)} fusion(s32[1,6,128]{2,1,0:T(8,128)} %bitcast.22, s32[1,6,128]{2,1,0:T(8,128)} %bitcast.23), kind=kLoop, calls=%fused_computation.30 | loop fusion | flops 1536 | bytes 12288 | tf_op jit(solution)/shard_map/stack | solution.py:470
  2.5 0.7 broadcast_multiply_fusion.4
  3.2 10.3 %shard_map.138 = s32[16,2,6,128]{3,2,1,0:T(8,128)} custom-call(s32[2,6,128]{2,1,0:T(8,128)} %pad_add_fusion.x_ref), custom_call_target="tpu_custom_call" | custom-call | tf_op jit(solution)/shard_map/pallas_call | solution.py:93
  13.5 0.9 fusion.5
  14.4 0.2 fusion
  14.7 0.1 slice.32
  14.8 0.2 subtract_reduce_fusion
  15.0 1.4 %convert_reduce_fusion.1 = (s32[]{:T(128)}, s32[16,768]{1,0:T(8,128)S(1)}) fusion(s32[]{:T(128)} %bitcast.2, f32[16,768]{1,0:T(8,128)S(1)} %fusion, f32[16]{0:T(128)S(1)} %subtract_reduce_fusion), kind=kLoop, calls=%fused_computation.18 | loop fusion | flops 61439 | bytes 98376 | tf_op jit(solution)/shard_map/reduce_sum | solution.py:198
  19.6 0.1 pad_dynamic-slice_fusion
  19.7 0.1 pad_dynamic-slice_fusion.1
  19.7 1.2 %convert_reduce_fusion = s32[1570]{0:T(1024)S(1)} fusion(s32[1570]{0:T(1024)S(1)} %pad_dynamic-slice_fusion.1, s32[1570]{0:T(1024)S(1)} %iota_add_fusion), kind=kLoop, calls=%fused_computation.2 | loop fusion | flops 7393130 | bytes 18840 | tf_op jit(solution)/shard_map/reduce_sum | solution.py:201
  21.0 1.7 %select_reduce_fusion = s32[1570]{0:T(1024)S(1)} fusion(s32[1571]{0:T(1024)S(1)} %pad_dynamic-slice_fusion, s32[1570]{0:T(1024)S(1)} %convert_reduce_fusion), kind=kLoop, calls=%fused_computation | loop fusion | flops 7397840 | bytes 18844 | tf_op jit(solution)/shard_map/reduce_sum | solution.py:204
  22.7 0.1 broadcast_multiply_fusion.1
  22.8 0.1 mul.77
  22.9 0.1 mul.75
  23.0 0.6 pad_maximum_fusion.2
  23.6 0.3 multiply_reduce_fusion
  23.9 0.1 fusion.1
  24.0 1.0 %pad_maximum_fusion.read_ref = bf16[800,240]{1,0:T(8,128)(2,1)} fusion(bf16[800,80]{1,0:T(8,128)(2,1)S(1)} %get-tuple-element.12, bf16[800,80]{1,0:T(8,128)(2,1)S(1)} %get-tuple-element.13), kind=kLoop, calls=%fused_computation.6 | loop fusion | flops 1152000 | bytes 640000 | tf_op jit(solution)/shard_map/concatenate | solution.py:234
  25.0 1.2 %broadcast_in_dim.20.ids_ref = s32[1792,1]{1,0:T(8,128)} reshape(s32[1792]{0:T(1024)S(1)} %concatenate.26) | data formatting | bytes 14336 | tf_op jit(solution)/shard_map/broadcast_in_dim | solution.py:208
  26.3 62.1 %shard_map.139 = (f32[8,1664]{1,0:T(8,128)}, f32[8,1664]{1,0:T(8,128)}, f32[24,512]{1,0:T(8,128)}, f32[32,1280]{1,0:T(8,128)}) custom-call(s32[1792,1]{1,0:T(8,128)} %broadcast_in_dim.20.ids_ref, bf16[1000,128]{1,0:T(8,128)(2,1)} %table_ref.1, bf16[384,512]{1,0:T(8,128)(2,1)} %pre_w.1, bf16[512,1280]{1,0:T(8,128)(2,1)} %up_w.1, f32[1,256]{1,0:T(1,128)} %bitcast.24, ...), custom_call_target="tpu_custom_call" | custom-call | tf_op jit(solution)/shard_map/pallas_call | solution.py:427
  88.3 0.9 fusion.2
  89.3 1.4 %broadcast_multiply_fusion.3 = f32[24,512]{1,0:T(8,128)} fusion(f32[24,512]{1,0:T(8,128)} %get-tuple-element.10), kind=kLoop, calls=%fused_computation.28 | loop fusion | flops 12288 | bytes 98304 | tf_op jit(solution)/shard_map/mul | solution.py:478
  90.7 1.6 %broadcast_multiply_fusion = f32[32,1280]{1,0:T(8,128)} fusion(f32[32,1280]{1,0:T(8,128)} %get-tuple-element.11), kind=kLoop, calls=%fused_computation.12 | loop fusion | flops 40960 | bytes 327680 | tf_op jit(solution)/shard_map/mul | solution.py:478
  92.3 0.3 copy.20
  92.6 1.2 %squeeze.12 = f32[7680]{0:T(1024)} reshape(f32[1,1536,5]{2,1,0:T(8,128)S(1)} %copy.20) | data formatting | bytes 61440 | tf_op jit(solution)/shard_map/squeeze | solution.py:478
  93.8 0.3 copy.19
  94.1 1.2 %squeeze.11 = f32[7680]{0:T(1024)} reshape(f32[1,1536,5]{2,1,0:T(8,128)S(1)} %copy.19) | data formatting | bytes 61440 | tf_op jit(solution)/shard_map/squeeze | solution.py:478
  (16 shorter events, 0.1 us)
Async XLA Ops:
  0.6 22.0 %copy-start.3 = (f32[5,5]{1,0:T(8,128)S(1)}, f32[5,5]{1,0:T(8,128)}, u32[]{:S(2)}) copy-start(f32[5,5]{1,0:T(8,128)} %constant.13.clone) | copy-start | bytes 304
  0.6 23.0 %copy-start = (f32[5,5,5,80]{3,2,1,0:T(8,128)S(1)}, f32[5,5,5,80]{3,2,1,0:T(8,128)}, u32[]{:S(2)}) copy-start(f32[5,5,5,80]{3,2,1,0:T(8,128)} %constant.55) | copy-start | bytes 120004
  0.7 22.0 %copy-start.2 = (f32[5,32]{1,0:T(8,128)S(1)}, f32[5,32]{1,0:T(8,128)}, u32[]{:S(2)}) copy-start(f32[5,32]{1,0:T(8,128)} %param.18) | copy-start | bytes 1924
  0.7 23.0 %copy-start.1 = (f32[5,5,32]{2,1,0:T(8,128)S(1)}, f32[5,5,32]{2,1,0:T(8,128)}, u32[]{:S(2)}) copy-start(f32[5,5,32]{2,1,0:T(8,128)} %param.17) | copy-start | bytes 9604

commit v2 on v1

--- a/solution.py
+++ b/solution.py
@@ -114,7 +114,7 @@
     nbits = n.bit_length() - 1
     first = tuple(range(nbits))
     second = (0,) + tuple(range(2, nbits)) + (1,)
-    orders = [second, first, second, first, second, first, second]
+    orders = [first, second] + [first] * 5
     return nbits, [stream_plan(nbits, order) for order in orders]
 
 
@@ -179,7 +179,7 @@
                 self.copy(s, t).wait_send()
 
 
-def frame_ids_of(gathered, total_frames):
+def unit_window(gathered, total_frames):
     n = gathered.shape[0]
     all_ids = gathered[:, 0].reshape(-1)
     dur_rows = gathered[:, 1].reshape(n, -1)
@@ -190,22 +190,14 @@
     row_total = within[:, row_units - 1]
     offsets = jnp.cumsum(row_total) - row_total
     unit_ends = (within + offsets[:, None]).reshape(-1).astype(jnp.int32)
-    width = EXT + 2
-    positions = lax.axis_index("tm") * F_DEV - HALO - 1 + jnp.arange(width, dtype=jnp.int32)
-    far_end = jnp.full((width,), total_frames + width, jnp.int32)
+    start = lax.axis_index("tm") * F_DEV - HALO - 1
+    far_end = jnp.full((LANES,), total_frames + LANES, jnp.int32)
     ends_padded = jnp.concatenate([unit_ends, far_end])
-    ids_padded = jnp.concatenate([all_ids, jnp.zeros((width + 1,), jnp.int32)])
-    first_unit = jnp.sum((unit_ends <= positions[0]).astype(jnp.int32))
-    window_ends = lax.dynamic_slice_in_dim(ends_padded, first_unit, width)
-    window_ids = lax.dynamic_slice_in_dim(ids_padded, first_unit, width + 1)
-    local_unit = jnp.sum((window_ends[None, :] <= positions[:, None]).astype(jnp.int32), axis=1)
-    slot_iota = jnp.arange(width + 1, dtype=jnp.int32)
-    picks = local_unit[:, None] == slot_iota[None, :]
-    frame_ids = jnp.sum(jnp.where(picks, window_ids[None, :], 0), axis=1)
-    inside = (positions >= 0) & (positions < total_frames)
-    frame_ids = jnp.where(inside, frame_ids, -1)
-    spare = FRONT * (-(-width // FRONT)) - width
-    return jnp.concatenate([frame_ids, jnp.full((spare,), -1, jnp.int32)])[:, None]
+    ids_padded = jnp.concatenate([all_ids, jnp.zeros((LANES,), jnp.int32)])
+    first_unit = jnp.sum((unit_ends <= start).astype(jnp.int32))
+    window_ends = lax.dynamic_slice_in_dim(ends_padded, first_unit, LANES)
+    window_ids = lax.dynamic_slice_in_dim(ids_padded, first_unit, LANES)
+    return window_ends[None, :], window_ids[None, :]
 
 
 def tap_places():
@@ -253,6 +245,7 @@
 
 def step_kernel(
     devices,
+    ends_ref,
     ids_ref,
     table_ref,
     pre_w,
@@ -293,16 +286,26 @@
     first_frame = lax.axis_index("tm") * F_DEV - HALO
     vocab = table_ref.shape[0]
 
+    ends = ends_ref[...]
+    slot = lax.broadcasted_iota(jnp.int32, (1, LANES), 1)
+    starts = jnp.where(slot == 0, -LANES, pltpu.roll(ends, 1, 1))
+
     def embed(i, carry):
         at = pl.multiple_of(i * FRONT, FRONT)
-        ids = ids_ref[pl.ds(at, FRONT), :]
-        one_hot = (ids == lax.broadcasted_iota(jnp.int32, (FRONT, vocab), 1)).astype(jnp.bfloat16)
+        row = lax.broadcasted_iota(jnp.int32, (FRONT, 1), 0)
+        position = row + (at + first_frame - 1)
+        owned = (starts <= position) & (position < ends)
+        ids = jnp.sum(jnp.where(owned, ids_ref[...], 0).astype(jnp.float32), axis=1, keepdims=True)
+        known = (position >= 0) & (position < total_frames)
+        ids = jnp.where(known, ids, -1.0)
+        places = lax.broadcasted_iota(jnp.int32, (FRONT, vocab), 1).astype(jnp.float32)
+        one_hot = (ids == places).astype(jnp.bfloat16)
         rows[pl.ds(at, FRONT), :] = jnp.dot(
             one_hot, table_ref[...], preferred_element_type=jnp.float32
         )
         return carry
 
-    lax.fori_loop(0, ids_ref.shape[0] // FRONT, embed, 0)
+    lax.fori_loop(0, rows.shape[0] // FRONT, embed, 0)
 
     columns[pl.ds(EXT, LANES - EXT), :] = jnp.zeros((LANES - EXT, 128), jnp.float32)
     lane = lax.broadcasted_iota(jnp.int32, (FRONT, 128), 1)
@@ -400,6 +403,8 @@
         slope = leaky_slope(pre_out[at : at + BACK, :].astype(jnp.float32))
         pre_grad[to : to + BACK, :] = (hidden * slope).astype(jnp.bfloat16)
     halving.advance(UP - 1, 0)
+    halving.advance(0, 1)
+    halving.advance(1, 1)
     for j in range(2):
         term = jnp.dot(
             window_t[...], pre_grad[:, C * j : C * (j + 1)], preferred_element_type=jnp.float32
@@ -408,15 +413,15 @@
     halving.advance(UP, 0)
     halving.advance(UP + 1, 0)
     for t in range(1, nbits):
-        for s in range(count):
+        for s in range(2 if t == 1 else 0, count):
             halving.advance(s, t)
     halving.finish()
 
 
-def step(frame_ids, unit_table, pre_weight, up_weight, post_weight, matrices, devices):
+def step(units, unit_table, pre_weight, up_weight, post_weight, matrices, devices):
     width, depth, span = up_weight.shape[1], up_weight.shape[0], pre_weight.shape[0]
     shape, bf16, f32 = jax.ShapeDtypeStruct, jnp.bfloat16, jnp.float32
-    operands = (frame_ids, unit_table, pre_weight, up_weight, post_weight[None, :], *matrices)
+    operands = (*units, unit_table, pre_weight, up_weight, post_weight[None, :], *matrices)
     nbits, plans = stream_plans(devices)
     terms, held, landed = [], [], []
     for s, plan in enumerate(plans):
@@ -435,7 +440,7 @@
         in_specs=[pl.BlockSpec(memory_space=VMEM)] * len(operands),
         out_specs=[pl.BlockSpec(memory_space=VMEM)] * 4,
         scratch_shapes=[
-            VMEM((frame_ids.shape[0], unit_table.shape[1]), f32),
+            VMEM((FRONT * (EXT // FRONT + 1), unit_table.shape[1]), f32),
             VMEM((EXT, span), bf16),
             VMEM((EXT, depth), bf16),
             VMEM((EXT, depth), bf16),
@@ -468,9 +473,9 @@
     total_samples = UP * total_frames
     matrices = disc_matrices(disc_taps, disc_out)
     gathered = gather_all(jnp.stack([unit_ids.reshape(-1, 128), durations.reshape(-1, 128)]), devices)
-    frame_ids = frame_ids_of(gathered, total_frames)
+    units = unit_window(gathered, total_frames)
     wave, wave_grad, grad_pre, grad_up = step(
-        frame_ids, unit_table, pre_weight, up_weight, post_weight, matrices, devices
+        units, unit_table, pre_weight, up_weight, post_weight, matrices, devices
     )
     mean_scale = 1.0 / total_samples
     both = jnp.stack([wave, wave_grad])[:, :UP, HALO : HALO + F_DEV]

time: 95.7 us -> 92.7 us (0.969)
  other arithmetic: 13.5 us -> 9.94 us
  Pallas kernels: 72.4 us -> 74.8 us
  between operations: 4.06 us -> 2.74 us
    reduce_sum x3 -> x1, other arithmetic: 4.26 us -> 0.73 us  [unit_window(): first_unit = jnp.sum((unit_ends <= start).astype(jnp.int32))]
    pallas_call x1, Pallas kernels: 62.1 us -> 64.5 us  [step(): pl.pallas_call(functools.partial(step_kernel, devices), out_shape=[shape(...]
where the time goes in v2:
time: 92.7 us; the launch traced here: 92.2 us
  Pallas kernels  74.8 us (81%)
  other arithmetic  9.94 us (11%)
  local copies, waits for them, and re-layouts  4.53 us (5%)
  between operations  2.74 us (3%)
    pallas_call x1, Pallas kernels, step(): pl.pallas_call(functools.partial(step_kernel, devices), out_shape=[shape(...  64.5 us
    pallas_call x1, Pallas kernels, gather_all(): pl.pallas_call(functools.partial(gather_kernel, n), out_shape=jax.ShapeDt...  10.3 us
    mul x2, other arithmetic, per_device(): return (both[0], both[1], grad_pre * mean_scale, grad_up * mean_scale)  3.02 us
    squeeze x2, local copies, waits for them, and re-layouts, per_device(): return (both[0], both[1], grad_pre * mean_scale, grad_up * mean_scale)  2.35 us

profile of v2, /device:TPU:0, one launch (start us, length us, event | category | flops | bytes accessed | tf_op | source)
XLA Modules:
  0.0 92.2 jit_solution(14650329473605348629)
XLA Ops:
  0.6 0.0 copy-start.3
  0.6 0.0 copy-start
  0.7 0.0 copy-start.2
  0.7 0.0 copy-start.1
  0.7 1.3 %pad_add_fusion.x_ref = s32[2,6,128]{2,1,0:T(8,128)} fusion(s32[1,6,128]{2,1,0:T(8,128)} %bitcast.21, s32[1,6,128]{2,1,0:T(8,128)} %bitcast.22), kind=kLoop, calls=%fused_computation.27 | loop fusion | flops 1536 | bytes 12288 | tf_op jit(solution)/shard_map/stack | solution.py:475
  2.0 0.7 broadcast_multiply_fusion.4
  2.8 10.3 %shard_map.138 = s32[16,2,6,128]{3,2,1,0:T(8,128)} custom-call(s32[2,6,128]{2,1,0:T(8,128)} %pad_add_fusion.x_ref), custom_call_target="tpu_custom_call" | custom-call | tf_op jit(solution)/shard_map/pallas_call | solution.py:93
  13.1 0.9 fusion.5
  14.0 0.2 fusion
  14.2 0.1 slice.28
  14.3 0.2 subtract_reduce_fusion
  14.5 0.7 convert_reduce_fusion
  17.2 0.1 pad_dynamic-slice_fusion
  17.3 0.6 broadcast_in_dim.7.ids_ref
  17.9 0.6 broadcast_in_dim.6.ends_ref
  18.5 0.0 copy-done.3
  18.5 0.1 broadcast_multiply_fusion.1
  18.6 0.1 mul.77
  18.7 0.1 mul.75
  18.8 0.6 pad_maximum_fusion.2
  19.4 0.0 copy-done
  19.4 0.3 multiply_reduce_fusion
  19.7 0.1 fusion.1
  19.8 1.0 %pad_maximum_fusion.read_ref = bf16[800,240]{1,0:T(8,128)(2,1)} fusion(bf16[800,80]{1,0:T(8,128)(2,1)S(1)} %get-tuple-element.12, bf16[800,80]{1,0:T(8,128)(2,1)S(1)} %get-tuple-element.13), kind=kLoop, calls=%fused_computation.3 | loop fusion | flops 1152000 | bytes 640000 | tf_op jit(solution)/shard_map/concatenate | solution.py:226
  20.8 64.5 %shard_map.139 = (f32[8,1664]{1,0:T(8,128)}, f32[8,1664]{1,0:T(8,128)}, f32[24,512]{1,0:T(8,128)}, f32[32,1280]{1,0:T(8,128)}) custom-call(s32[1,1664]{1,0:T(1,128)} %broadcast_in_dim.6.ends_ref, s32[1,1664]{1,0:T(1,128)} %broadcast_in_dim.7.ids_ref, bf16[1000,128]{1,0:T(8,128)(2,1)} %table_ref.1, bf16[384,512]{1,0:T(8,128)(2,1)} %pre_w.1, ...), custom_call_target="tpu_custom_call" | custom-call | tf_op jit(solution)/shard_map/pallas_call | solution.py:432
  85.3 0.9 fusion.2
  86.3 1.4 %broadcast_multiply_fusion.3 = f32[24,512]{1,0:T(8,128)} fusion(f32[24,512]{1,0:T(8,128)} %get-tuple-element.10), kind=kLoop, calls=%fused_computation.25 | loop fusion | flops 12288 | bytes 98304 | tf_op jit(solution)/shard_map/mul | solution.py:483
  87.7 1.6 %broadcast_multiply_fusion = f32[32,1280]{1,0:T(8,128)} fusion(f32[32,1280]{1,0:T(8,128)} %get-tuple-element.11), kind=kLoop, calls=%fused_computation.9 | loop fusion | flops 40960 | bytes 327680 | tf_op jit(solution)/shard_map/mul | solution.py:483
  89.3 0.3 copy.18
  89.6 1.2 %squeeze.8 = f32[7680]{0:T(1024)} reshape(f32[1,1536,5]{2,1,0:T(8,128)S(1)} %copy.18) | data formatting | bytes 61440 | tf_op jit(solution)/shard_map/squeeze | solution.py:483
  90.8 0.3 copy.17
  91.1 1.2 %squeeze.7 = f32[7680]{0:T(1024)} reshape(f32[1,1536,5]{2,1,0:T(8,128)S(1)} %copy.17) | data formatting | bytes 61440 | tf_op jit(solution)/shard_map/squeeze | solution.py:483
  (10 shorter events, 0.1 us)
Async XLA Ops:
  0.6 17.8 %copy-start.3 = (f32[5,5]{1,0:T(8,128)S(1)}, f32[5,5]{1,0:T(8,128)}, u32[]{:S(2)}) copy-start(f32[5,5]{1,0:T(8,128)} %constant.35.clone) | copy-start | bytes 304
  0.6 18.8 %copy-start = (f32[5,5,5,80]{3,2,1,0:T(8,128)S(1)}, f32[5,5,5,80]{3,2,1,0:T(8,128)}, u32[]{:S(2)}) copy-start(f32[5,5,5,80]{3,2,1,0:T(8,128)} %constant.45) | copy-start | bytes 120004
  0.7 17.8 %copy-start.2 = (f32[5,32]{1,0:T(8,128)S(1)}, f32[5,32]{1,0:T(8,128)}, u32[]{:S(2)}) copy-start(f32[5,32]{1,0:T(8,128)} %param.18) | copy-start | bytes 1924
  0.7 18.8 %copy-start.1 = (f32[5,5,32]{2,1,0:T(8,128)S(1)}, f32[5,5,32]{2,1,0:T(8,128)}, u32[]{:S(2)}) copy-start(f32[5,5,32]{2,1,0:T(8,128)} %param.17) | copy-start | bytes 9604
